TPU v7x, 32 devices: a whole 2x2x4 slice. The times are simulated.
32 devices in a mesh: area: 8 (over y, x, core), layer: 4 (over z).
Axes of the slice: x: 2, y: 2, z: 4, core: 2. Of those that a mesh axis runs over, the one named last changes fastest.
Arguments:
- permeability: float32 [16, 4096, 512], P('layer', 'area'), may hold values from 0.1 to 10
- mobility: float32 [16, 4096, 512], P('layer', 'area'), may hold values from 0.3 to 3
- thickness: float32 [16], P('layer'), may hold values from 0.5 to 2
- caprock: int32 [4096, 512], P('area'), may hold values from 0 to 7
- plume: int32 [4096, 512], P('area'), may hold values from 0 to 15
- storage: float32 [4096, 512], P('area'), may hold values from 1.6 to 16
- source: float32 [4096, 512], P('area'), may hold values from -192 to 192
- pressure_old: float32 [4096, 512], P('area'), may hold values from -6 to 6
Outputs:
- cell_pressure: float32 [16, 4096, 512], P('layer', 'area')
- flux_rows: float32 [16, 4096, 512], P('layer', 'area')
- flux_cols: float32 [16, 4096, 512], P('layer', 'area')
Inputs may be any that keep to these rules, and one draw needn't show every extreme that they name: Layers above layer caprock of a column are sealed rock. CO2 fills the open layers above layer plume of a column; where plume <= caprock a column holds no CO2.
All inputs are finite; a program needn't handle non-finite values.
Results may differ from a plain program's by a relative error of at most 0.0003.
Values sent between devices are 32-bit elements; how exact they have to be, the bound alone decides.
No kernel may reach another device: no remote copies, remote signals or barrier semaphores. Data moves between devices by JAX's collectives and lax.ppermute only.
A program may use at most 128 MiB of HBM per device.

v0:
```python
import jax
import jax.numpy as jnp
from jax import lax
from jax.sharding import PartitionSpec as P

SWEEPS = 3
buoyancy_scale = 0.3
gravity_scale = 0.05
gas_density = 0.7
brine_density = 1.0


def padded_2(block, sides, width):
    for axis, dim in sides:
        count = lax.axis_size(axis)
        forward = [(i, i + 1) for i in range(count - 1)]
        backward = [(target, source) for source, target in forward]
        low = lax.ppermute(
            lax.slice_in_dim(block, block.shape[dim] - width, None, axis=dim), axis, forward
        )
        high = lax.ppermute(lax.slice_in_dim(block, 0, width, axis=dim), axis, backward)
        block = jnp.concatenate([low, block, high], axis=dim)
    return block


def from_behind(block, axis, distance):
    devices = range(lax.axis_size(axis))
    route = [(i - distance, i) for i in devices if i - distance in devices]
    return lax.ppermute(block, axis, route)


def harmonic(near_value, far_value):
    summed = near_value + far_value
    divisor = jnp.where(summed > 0, summed, 1.0)
    return 2.0 * near_value * far_value / divisor


def neighbours(padded, row_count):
    widened = jnp.pad(padded, ((0, 0), (1, 1)))
    return [
        widened[0:row_count, 1:-1],
        widened[2 : row_count + 2, 1:-1],
        widened[1 : row_count + 1, 0:-2],
        widened[1 : row_count + 1, 2:],
    ]


def prepare(summed_pad, storage, source, pressure_old):
    row_count = storage.shape[0]
    trans_pad = summed_pad[0]
    buoy_pad = summed_pad[1]
    drive_pad = buoyancy_scale * summed_pad[2]
    trans_faces = [
        harmonic(trans_pad[1 : row_count + 1], neighbour)
        for neighbour in neighbours(trans_pad, row_count)
    ]
    buoy_faces = [
        harmonic(buoy_pad[1 : row_count + 1], neighbour)
        for neighbour in neighbours(buoy_pad, row_count)
    ]
    drive_centre = drive_pad[1 : row_count + 1]
    gravity_drive = sum(
        (
            face_coef * (neighbour - drive_centre)
            for face_coef, neighbour in zip(buoy_faces, neighbours(drive_pad, row_count))
        )
    )
    right_hand = storage * pressure_old + source + gravity_drive
    diagonal = storage + trans_faces[0] + trans_faces[1] + trans_faces[2] + trans_faces[3]
    return (trans_faces, right_hand, diagonal)


def relax(trans_faces, right_hand, diagonal, padded):
    row_count = right_hand.shape[0]
    inflow = sum(
        (
            face_coef * neighbour
            for face_coef, neighbour in zip(trans_faces, neighbours(padded, row_count))
        )
    )
    return (right_hand + inflow) / diagonal


def column_depths(every_thick, layer_count, caprock, plume, limit):
    block_count = every_thick.shape[0] // layer_count

    def add_block(block, carry):
        height, above = carry
        first = block * layer_count
        thick_block = lax.dynamic_slice_in_dim(every_thick, first, layer_count, 0)[:, None, None]
        depth = first + lax.broadcasted_iota(jnp.int32, (layer_count, 1, 1), 0)
        gas = (depth >= caprock[None]) & (depth < plume[None])
        height = height + jnp.sum(jnp.where(gas, thick_block, 0.0), axis=0)
        above = above + jnp.sum(jnp.where(gas & (depth < limit), thick_block, 0.0), axis=0)
        return (height, above)

    zeros = jnp.zeros(caprock.shape, jnp.float32)
    return lax.fori_loop(0, block_count, add_block, (zeros, zeros))


def local(permeability, mobility, thickness, caprock, plume, storage, source, pressure_old):
    layer_count = permeability.shape[0]
    layer_index = lax.axis_index("layer")
    layers = layer_index * layer_count + lax.broadcasted_iota(jnp.int32, permeability.shape, 0)
    open_cell = layers >= caprock[None]
    gas_cell = open_cell & (layers < plume[None])
    layer_thick = thickness[:, None, None]
    conduct = jnp.where(open_cell, permeability * mobility * layer_thick, 0.0)
    every_thick = lax.all_gather(thickness, "layer", axis=0, tiled=True)
    limit = layer_index * layer_count
    gas_height, gas_above = column_depths(every_thick, layer_count, caprock, plume, limit)
    column_parts = jnp.stack(
        [jnp.sum(conduct, axis=0), jnp.sum(jnp.where(gas_cell, conduct, 0.0), axis=0)]
    )
    summed = lax.psum(column_parts, "layer")
    summed = jnp.concatenate([summed, gas_height[None]], axis=0)
    padded = padded_2(summed, (("area", 1),), 1)
    trans_faces, right_hand, diagonal = prepare(padded, storage, source, pressure_old)
    pressure = pressure_old
    for sweep_index in range(SWEEPS):
        pressure_pad = padded_2(pressure, (("area", 0),), 1)
        pressure = relax(trans_faces, right_hand, diagonal, pressure_pad)
    layer_mass = layer_thick * jnp.where(gas_cell, gas_density, brine_density)
    depth_all = lax.broadcasted_iota(jnp.int32, every_thick.shape, 0)
    thick_over = jnp.sum(jnp.where(depth_all < limit, every_thick, 0.0))
    mass_over = thick_over - (brine_density - gas_density) * gas_above
    hydro_head = mass_over[None] + jnp.cumsum(layer_mass, axis=0) - 0.5 * layer_mass
    cell_pressure = pressure[None] + gravity_scale * hydro_head
    edge_rows = jnp.stack([conduct[:, 0, :], cell_pressure[:, 0, :]])
    beyond = from_behind(edge_rows, "area", -1)
    next_conduct = jnp.concatenate([conduct[:, 1:, :], beyond[0][:, None, :]], axis=1)
    next_pressure = jnp.concatenate([cell_pressure[:, 1:, :], beyond[1][:, None, :]], axis=1)
    flux_rows = harmonic(conduct, next_conduct) * (cell_pressure - next_pressure)
    side_conduct = jnp.pad(conduct[:, :, 1:], ((0, 0), (0, 0), (0, 1)))
    side_pressure = jnp.pad(cell_pressure[:, :, 1:], ((0, 0), (0, 0), (0, 1)))
    flux_cols = harmonic(conduct, side_conduct) * (cell_pressure - side_pressure)
    return (cell_pressure, flux_rows, flux_cols)


def solution(mesh):
    in_specs = (
        P("layer", "area", None),
        P("layer", "area", None),
        P("layer"),
        P("area", None),
        P("area", None),
        P("area", None),
        P("area", None),
        P("area", None),
    )
    out_specs = (P("layer", "area", None), P("layer", "area", None), P("layer", "area", None))
    return jax.shard_map(local, mesh=mesh, in_specs=in_specs, out_specs=out_specs, check_vma=False)
```

profile of v0, /device:TPU:4, one launch (start us, length us, event | category | flops | bytes accessed | tf_op | source)
XLA Modules:
  0.0 176.6 jit_solution(2895812345910085846)
XLA Ops:
  8.0 1.9 %collective-permute-start.2 = (f32[1,512]{1,0:T(1,128)S(1)}, f32[1,512]{1,0:T(1,128)S(1)}, u32[]{:S(2)}, u32[]{:S(2)}) collective-permute-start(f32[1,512]{1,0:T(1,128)S(1)} %get-tuple-element.191), channel_id=1, source_target_pairs={{0,4},{4,8},{8,12},{12,16},{16,20},{20,24},{24,28},{1,5},{5,9},{9,... | collective-permute-start | bytes 6152 | tf_op jit(solution)/shard_map/ppermute | solution.py:18
  9.9 4.5 %collective-permute-start.3 = (f32[1,512]{1,0:T(1,128)S(1)}, f32[1,512]{1,0:T(1,128)S(1)}, u32[]{:S(2)}, u32[]{:S(2)}) collective-permute-start(f32[1,512]{1,0:T(1,128)S(1)} %get-tuple-element.192), channel_id=1, source_target_pairs={{4,0},{8,4},{12,8},{16,12},{20,16},{24,20},{28,24},{5,1},{9,5},{13... | collective-permute-start | bytes 6152 | tf_op jit(solution)/shard_map/ppermute | solution.py:21
  14.4 7.8 %fusion.59 = (f32[512,512]{1,0:T(8,128)S(1)}, f32[512,512]{1,0:T(8,128)S(1)}, f32[4,512,512]{2,1,0:T(8,128)}) fusion(s32[512,512]{1,0:T(8,128)} %param.14, s32[512,512]{1,0:T(8,128)} %param.13, s32[4]{0:T(128)S(1)} %iota_add_fusion.1, f32[4]{0:T(128)} %param.12, f32[4,512,512]{2,1,0:T(8,128)} %param.10, f32[4,512,512]{2,1,0:T(8,128)} %param.11), kind=kLoop, calls=%fused_computation.138 | loop fusion | flops 8912896 | bytes 16777248 | tf_op jit(solution)/shard_map/reduce_sum | solution.py:113
  22.2 1.5 pad_maximum_fusion.2
  25.2 12.4 %all-reduce.8 = f32[16]{0:T(128)S(1)} all-reduce(f32[16]{0:T(128)S(1)} %dynamic-update-slice), channel_id=1, replica_groups=mesh['area'=8,'layer'=4] {'layer'}, use_global_device_ids=true, to_apply=%add.8 | all-reduce | flops 16 | bytes 128
  37.6 12.6 %while.16 = (s32[]{:T(128)}, f32[512,512]{1,0:T(8,128)S(1)}, f32[512,512]{1,0:T(8,128)}, s32[512,512]{1,0:T(8,128)S(1)}, s32[512,512]{1,0:T(8,128)S(1)}, /*index...) while((s32[]{:T(128)}, f32[512,512]{1,0:T(8,128)S(1)}, ...), condition=%wide.region_6.7_spmd.clone, body=%wide.region_3.0_spmd.clone.sunk | while | flops 8912915 | bytes 18874700 | solution.py:98
  37.7 1.3 select_reduce_fusion.4
  40.8 1.3 select_reduce_fusion.4
  50.8 59.5 %all-reduce.11.cloned.1.call-done = f32[2,512,512]{2,1,0:T(8,128)} async-done(((f32[2,512,512]{2,1,0:T(8,128)}), f32[2,512,512]{2,1,0:T(8,128)}) %all-reduce.11.cloned.1.call-update) | async-done | bytes 2097168 | tf_op jit(solution)/shard_map/psum | solution.py:115
  111.3 1.9 %collective-permute-start = (f32[3,1,512]{2,1,0:T(1,128)S(1)}, f32[3,1,512]{2,1,0:T(1,128)S(1)}, u32[]{:S(2)}, u32[]{:S(2)}) collective-permute-start(f32[3,1,512]{2,1,0:T(1,128)S(1)} %get-tuple-element.185), channel_id=1, source_target_pairs={{0,4},{4,8},{8,12},{12,16},{16,20},{20,24},{24,28},{1,5},{5,9},{9,... | collective-permute-start | bytes 18440 | tf_op jit(solution)/shard_map/ppermute | solution.py:18
  113.2 4.5 %collective-permute-start.1 = (f32[3,1,512]{2,1,0:T(1,128)S(1)}, f32[3,1,512]{2,1,0:T(1,128)S(1)}, u32[]{:S(2)}, u32[]{:S(2)}) collective-permute-start(f32[3,1,512]{2,1,0:T(1,128)S(1)} %get-tuple-element.186), channel_id=1, source_target_pairs={{4,0},{8,4},{12,8},{16,12},{20,16},{24,20},{28,24},{5,1},{9,5},{13... | collective-permute-start | bytes 18440 | tf_op jit(solution)/shard_map/ppermute | solution.py:21
  117.8 1.6 select_maximum_fusion.4
  121.8 6.4 %fusion.46 = (f32[512,512]{1,0:T(8,128)S(1)}, f32[512,512]{1,0:T(8,128)S(1)}, f32[512,512]{1,0:T(8,128)S(1)}, f32[512,512]{1,0:T(8,128)S(1)}) fusion(f32[514,514]{1,0:T(8,128)S(1)} %select_maximum_fusion.4, f32[1,512]{1,0:T(1,128)S(1)} %collective-permute-done.3, f32[512,512]{1,0:T(8,128)S(1)} %copy-done.9, f32[1,512]{1,0:T(1,128)S(1)} %collective-permute-done.2, ...), kind=kLoop, calls=%fused_computation.98 | loop fusion | flops 20709376 | bytes 21037056 | tf_op jit(solution)/shard_map/div | solution.py:81
  128.2 2.2 %collective-permute-start.4 = (f32[1,512]{1,0:T(1,128)S(1)}, f32[1,512]{1,0:T(1,128)S(1)}, u32[]{:S(2)}, u32[]{:S(2)}) collective-permute-start(f32[1,512]{1,0:T(1,128)S(1)} %get-tuple-element.189), channel_id=1, source_target_pairs={{0,4},{4,8},{8,12},{12,16},{16,20},{20,24},{24,28},{1,5},{5,9},{9,... | collective-permute-start | bytes 6152 | tf_op jit(solution)/shard_map/ppermute | solution.py:18
  130.4 4.3 %collective-permute-start.5 = (f32[1,512]{1,0:T(1,128)S(1)}, f32[1,512]{1,0:T(1,128)S(1)}, u32[]{:S(2)}, u32[]{:S(2)}) collective-permute-start(f32[1,512]{1,0:T(1,128)S(1)} %get-tuple-element.190), channel_id=1, source_target_pairs={{4,0},{8,4},{12,8},{16,12},{20,16},{24,20},{28,24},{5,1},{9,5},{13... | collective-permute-start | bytes 6152 | tf_op jit(solution)/shard_map/ppermute | solution.py:21
  136.4 1.7 fusion.39
  138.2 1.9 %collective-permute-start.6 = (f32[1,512]{1,0:T(1,128)S(1)}, f32[1,512]{1,0:T(1,128)S(1)}, u32[]{:S(2)}, u32[]{:S(2)}) collective-permute-start(f32[1,512]{1,0:T(1,128)S(1)} %get-tuple-element.187), channel_id=1, source_target_pairs={{0,4},{4,8},{8,12},{12,16},{16,20},{20,24},{24,28},{1,5},{5,9},{9,... | collective-permute-start | bytes 6152 | tf_op jit(solution)/shard_map/ppermute | solution.py:18
  140.1 4.7 %collective-permute-start.7 = (f32[1,512]{1,0:T(1,128)S(1)}, f32[1,512]{1,0:T(1,128)S(1)}, u32[]{:S(2)}, u32[]{:S(2)}) collective-permute-start(f32[1,512]{1,0:T(1,128)S(1)} %get-tuple-element.188), channel_id=1, source_target_pairs={{4,0},{8,4},{12,8},{16,12},{20,16},{24,20},{28,24},{5,1},{9,5},{13... | collective-permute-start | bytes 6152 | tf_op jit(solution)/shard_map/ppermute | solution.py:21
  146.4 1.7 fusion.32
  148.1 2.2 %multiply_add_fusion = f32[4,512,512]{2,1,0:T(8,128)S(1)} fusion(f32[512,512]{1,0:T(8,128)S(1)} %multiply_subtract_fusion, f32[512,512]{1,0:T(8,128)S(1)} %fusion.32, s32[512,512]{1,0:T(8,128)S(1)} %get-tuple-element.281, f32[4]{0:T(128)S(1)} %copy-done.11, s32[512,512]{1,0:T(8,128)S(1)} %get-tuple-element.280, s32[4]{0:T(128)S(1)} %iota_add_fusion.1), kind=kOutput, calls=%fused_computation.17 | output fusion | flops 18874368 | bytes 8388640 | tf_op jit(solution)/shard_map/jit(cumsum)/reduce_window_sum | solution.py:127
  150.3 4.5 %collective-permute-start.8 = (f32[2,4,512]{2,0,1:T(2,128)S(1)}, f32[2,4,512]{2,0,1:T(2,128)S(1)}, u32[]{:S(2)}, u32[]{:S(2)}) collective-permute-start(f32[2,4,512]{2,0,1:T(2,128)S(1)} %pad_maximum_fusion.13), channel_id=1, source_target_pairs={{4,0},{8,4},{12,8},{16,12},{20,16},{24,20},{28,24},{5,1},{9,5},{13... | collective-permute-start | bytes 49160 | tf_op jit(solution)/shard_map/ppermute | solution.py:29
  156.6 3.1 %slice.283 = f32[4,512,511]{2,1,0:T(8,128)} slice(f32[4,512,512]{2,1,0:T(8,128)S(1)} %multiply_add_fusion), slice={[0:4], [0:512], [1:512]} | slice | bytes 8372224 | tf_op jit(solution)/shard_map/slice | solution.py:135
  159.7 2.5 %slice.280 = f32[4,511,512]{2,1,0:T(8,128)} slice(f32[4,512,512]{2,1,0:T(8,128)S(1)} %multiply_add_fusion), slice={[0:4], [1:512], [0:512]} | slice | bytes 8372224 | tf_op jit(solution)/shard_map/slice | solution.py:132
  162.3 7.4 %fusion.3 = (f32[4,512,512]{2,1,0:T(8,128)}, f32[4,512,512]{2,1,0:T(8,128)}) fusion(f32[4,512,512]{2,1,0:T(8,128)S(1)} %multiply_add_fusion, f32[4,512,511]{2,1,0:T(8,128)} %slice.283, f32[4,512,512]{2,1,0:T(8,128)S(1)} %copy-done.1, f32[4,512,511]{2,1,0:T(8,128)S(1)} %slice.282, f32[4,1,512]{2,1,0:T(1,128)S(1)} %get-tuple-element.194, ...), kind=kLoop, calls=%fused_computation.14 | loop fusion | flops 17825792 | bytes 33538048 | tf_op jit(solution)/shard_map/mul | solution.py:136
  (89 shorter events, 20.3 us)
Async XLA Ops:
  7.2 103.2 %all-reduce.11.cloned.1.call-start = ((), (), s32[]{:S(2)}) async-start(), calls=%async_computation | async-start | bytes 4194304 | tf_op jit(solution)/shard_map/psum | solution.py:115
  8.0 109.8 %collective-permute-start.2 = (f32[1,512]{1,0:T(1,128)S(1)}, f32[1,512]{1,0:T(1,128)S(1)}, u32[]{:S(2)}, u32[]{:S(2)}) collective-permute-start(f32[1,512]{1,0:T(1,128)S(1)} %get-tuple-element.191), channel_id=1, source_target_pairs={{0,4},{4,8},{8,12},{12,16},{16,20},{20,24},{24,28},{1,5},{5,9},{9,... | collective-permute-start | bytes 6152 | tf_op jit(solution)/shard_map/ppermute | solution.py:18
  9.9 107.9 %collective-permute-start.3 = (f32[1,512]{1,0:T(1,128)S(1)}, f32[1,512]{1,0:T(1,128)S(1)}, u32[]{:S(2)}, u32[]{:S(2)}) collective-permute-start(f32[1,512]{1,0:T(1,128)S(1)} %get-tuple-element.192), channel_id=1, source_target_pairs={{4,0},{8,4},{12,8},{16,12},{20,16},{24,20},{28,24},{5,1},{9,5},{13... | collective-permute-start | bytes 6152 | tf_op jit(solution)/shard_map/ppermute | solution.py:21
  22.2 1.6 copy-start.12
  22.2 2.7 %copy-start.11 = (f32[4]{0:T(128)S(1)}, f32[4]{0:T(128)}, u32[]{:S(2)}) copy-start(f32[4]{0:T(128)} %param.12) | copy-start | bytes 52
  22.2 15.4 %copy-start.2 = (s32[512,512]{1,0:T(8,128)S(1)}, s32[512,512]{1,0:T(8,128)}, u32[]{:S(2)}) copy-start(s32[512,512]{1,0:T(8,128)} %param.13) | copy-start | bytes 3145732
  22.2 15.4 %copy-start.3 = (s32[512,512]{1,0:T(8,128)S(1)}, s32[512,512]{1,0:T(8,128)}, u32[]{:S(2)}) copy-start(s32[512,512]{1,0:T(8,128)} %param.14) | copy-start | bytes 3145732
  37.6 1.4 copy-start.5
  40.8 1.4 copy-start.5
  43.9 1.4 copy-start.5
  47.0 1.4 copy-start.5
  110.3 9.1 %copy-start.4 = (f32[2,512,512]{2,1,0:T(8,128)S(1)}, f32[2,512,512]{2,1,0:T(8,128)}, u32[]{:S(2)}) copy-start(f32[2,512,512]{2,1,0:T(8,128)} %all-reduce.11.cloned.1.call-done) | copy-start | bytes 6291460
  111.3 8.2 %collective-permute-start = (f32[3,1,512]{2,1,0:T(1,128)S(1)}, f32[3,1,512]{2,1,0:T(1,128)S(1)}, u32[]{:S(2)}, u32[]{:S(2)}) collective-permute-start(f32[3,1,512]{2,1,0:T(1,128)S(1)} %get-tuple-element.185), channel_id=1, source_target_pairs={{0,4},{4,8},{8,12},{12,16},{16,20},{20,24},{24,28},{1,5},{5,9},{9,... | collective-permute-start | bytes 18440 | tf_op jit(solution)/shard_map/ppermute | solution.py:18
  113.2 6.2 %collective-permute-start.1 = (f32[3,1,512]{2,1,0:T(1,128)S(1)}, f32[3,1,512]{2,1,0:T(1,128)S(1)}, u32[]{:S(2)}, u32[]{:S(2)}) collective-permute-start(f32[3,1,512]{2,1,0:T(1,128)S(1)} %get-tuple-element.186), channel_id=1, source_target_pairs={{4,0},{8,4},{12,8},{16,12},{20,16},{24,20},{28,24},{5,1},{9,5},{13... | collective-permute-start | bytes 18440 | tf_op jit(solution)/shard_map/ppermute | solution.py:21
  119.9 1.5 copy-start.9
  119.9 1.8 %copy-start.10 = (f32[512,512]{1,0:T(8,128)S(1)}, f32[512,512]{1,0:T(8,128)}, u32[]{:S(2)}) copy-start(f32[512,512]{1,0:T(8,128)} %param.16) | copy-start | bytes 3145732
  121.8 12.9 %copy-start.7 = (f32[512,512]{1,0:T(8,128)S(1)}, f32[512,512]{1,0:T(8,128)}, u32[]{:S(2)}) copy-start(f32[512,512]{1,0:T(8,128)} %get-tuple-element.129) | copy-start | bytes 3145732
  128.2 7.2 %collective-permute-start.4 = (f32[1,512]{1,0:T(1,128)S(1)}, f32[1,512]{1,0:T(1,128)S(1)}, u32[]{:S(2)}, u32[]{:S(2)}) collective-permute-start(f32[1,512]{1,0:T(1,128)S(1)} %get-tuple-element.189), channel_id=1, source_target_pairs={{0,4},{4,8},{8,12},{12,16},{16,20},{20,24},{24,28},{1,5},{5,9},{9,... | collective-permute-start | bytes 6152 | tf_op jit(solution)/shard_map/ppermute | solution.py:18
  130.4 5.6 %collective-permute-start.5 = (f32[1,512]{1,0:T(1,128)S(1)}, f32[1,512]{1,0:T(1,128)S(1)}, u32[]{:S(2)}, u32[]{:S(2)}) collective-permute-start(f32[1,512]{1,0:T(1,128)S(1)} %get-tuple-element.190), channel_id=1, source_target_pairs={{4,0},{8,4},{12,8},{16,12},{20,16},{24,20},{28,24},{5,1},{9,5},{13... | collective-permute-start | bytes 6152 | tf_op jit(solution)/shard_map/ppermute | solution.py:21
  136.4 8.4 %copy-start.1 = (f32[4,512,512]{2,1,0:T(8,128)S(1)}, f32[4,512,512]{2,1,0:T(8,128)}, u32[]{:S(2)}) copy-start(f32[4,512,512]{2,1,0:T(8,128)} %get-tuple-element.176) | copy-start | bytes 12582916
  138.2 6.7 %collective-permute-start.6 = (f32[1,512]{1,0:T(1,128)S(1)}, f32[1,512]{1,0:T(1,128)S(1)}, u32[]{:S(2)}, u32[]{:S(2)}) collective-permute-start(f32[1,512]{1,0:T(1,128)S(1)} %get-tuple-element.187), channel_id=1, source_target_pairs={{0,4},{4,8},{8,12},{12,16},{16,20},{20,24},{24,28},{1,5},{5,9},{9,... | collective-permute-start | bytes 6152 | tf_op jit(solution)/shard_map/ppermute | solution.py:18
  140.1 5.8 %collective-permute-start.7 = (f32[1,512]{1,0:T(1,128)S(1)}, f32[1,512]{1,0:T(1,128)S(1)}, u32[]{:S(2)}, u32[]{:S(2)}) collective-permute-start(f32[1,512]{1,0:T(1,128)S(1)} %get-tuple-element.188), channel_id=1, source_target_pairs={{4,0},{8,4},{12,8},{16,12},{20,16},{24,20},{28,24},{5,1},{9,5},{13... | collective-permute-start | bytes 6152 | tf_op jit(solution)/shard_map/ppermute | solution.py:21
  150.3 12.0 %copy-start = (f32[4,512,512]{2,1,0:T(8,128)}, f32[4,512,512]{2,1,0:T(8,128)S(1)}, u32[]{:S(2)}) copy-start(f32[4,512,512]{2,1,0:T(8,128)S(1)} %multiply_add_fusion) | copy-start | bytes 12582916
  150.3 11.9 %collective-permute-start.8 = (f32[2,4,512]{2,0,1:T(2,128)S(1)}, f32[2,4,512]{2,0,1:T(2,128)S(1)}, u32[]{:S(2)}, u32[]{:S(2)}) collective-permute-start(f32[2,4,512]{2,0,1:T(2,128)S(1)} %pad_maximum_fusion.13), channel_id=1, source_target_pairs={{4,0},{8,4},{12,8},{16,12},{20,16},{24,20},{28,24},{5,1},{9,5},{13... | collective-permute-start | bytes 49160 | tf_op jit(solution)/shard_map/ppermute | solution.py:29
  (5 other events, 5.1 us)
Sparse Core Ops, SparseCore 0:
  23.9 86.4 all-reduce.10
where the time goes:
time: 177 us
  waiting for transfers between devices  61.2 us (35%)
  other arithmetic  42.7 us (24%)
  starting transfers between devices  30.6 us (17%)
  between operations  15 us (8%)
  local copies, waits for them, and re-layouts  14.7 us (8%)
  blocking collectives  12.4 us (7%)
    psum x1, waiting for transfers between devices, local(): summed = lax.psum(column_parts, 'layer')  59.5 us
    ppermute x4, starting transfers between devices, padded_2(): lax.ppermute(lax.slice_in_dim(block, 0, width, axis=dim), axis, backward)  18.1 us
    unnamed x1, blocking collectives  12.4 us
    div x3, other arithmetic, relax(): return (right_hand + inflow) / diagonal  9.84 us
    ppermute x4, starting transfers between devices, padded_2(): lax.ppermute(lax.slice_in_dim(block, block.shape[dim] - width, None, axis...  7.92 us
    reduce_sum x1, other arithmetic, local(): jnp.sum(conduct, axis=0)  7.77 us
    mul x1, other arithmetic, local(): harmonic(conduct, side_conduct) * (cell_pressure - side_pressure)  7.44 us
    reduce_sum x4, other arithmetic, add_block(): jnp.sum(jnp.where(gas & (depth < limit), thick_block, 0.0), axis=0)  5.35 us
  transfers between devices with their start and end apart: 10, of which 3 were waited for; matrix products, arithmetic and copies ran while one was open for 17% of the time, Pallas kernels for 0%

commit v1 on v0

--- a/solution.py
+++ b/solution.py
@@ -112,7 +112,9 @@
     column_parts = jnp.stack(
         [jnp.sum(conduct, axis=0), jnp.sum(jnp.where(gas_cell, conduct, 0.0), axis=0)]
     )
-    summed = lax.psum(column_parts, "layer")
+    summed = column_parts
+    for hop in (1, 2):
+        summed = summed + lax.ppermute(summed, "layer", [(dev, dev ^ hop) for dev in range(4)])
     summed = jnp.concatenate([summed, gas_height[None]], axis=0)
     padded = padded_2(summed, (("area", 1),), 1)
     trans_faces, right_hand, diagonal = prepare(padded, storage, source, pressure_old)

time: 177 us -> 221 us (1.25)
  blocking collectives: 12.4 us -> 42.7 us
  waiting for transfers between devices: 61.2 us -> 80.5 us
  between operations: 15 us -> 1.66 us
  other arithmetic: 42.7 us -> 48 us
    ppermute x0 -> x2, waiting for transfers between devices: none -> 78 us  [local(): lax.ppermute(summed, 'layer', [(dev, dev ^ hop) for dev in range(4)])]
    psum x1 -> x0, waiting for transfers between devices: 59.5 us -> none  [local(): summed = lax.psum(column_parts, 'layer')]
    unnamed x1, blocking collectives: 12.4 us -> 42.7 us
    add x0 -> x2, other arithmetic: none -> 7.52 us  [local(): summed + lax.ppermute(summed, 'layer', [(dev, dev ^ hop) for dev in range...]
  transfers between devices with their start and end apart: 10 -> 11, of which waited for: 3 -> 4; matrix products, arithmetic and copies ran while one was open for 17% -> 12% of each run, Pallas kernels for 0% -> 0%
where the time goes in v1:
time: 221 us
  waiting for transfers between devices  80.5 us (36%)
  other arithmetic  48 us (22%)
  blocking collectives  42.7 us (19%)
  starting transfers between devices  32.2 us (15%)
  local copies, waits for them, and re-layouts  15.4 us (7%)
    ppermute x2, waiting for transfers between devices, local(): lax.ppermute(summed, 'layer', [(dev, dev ^ hop) for dev in range(4)])  78 us
    unnamed x1, blocking collectives  42.7 us
    ppermute x4, starting transfers between devices, padded_2(): lax.ppermute(lax.slice_in_dim(block, 0, width, axis=dim), axis, backward)  17.7 us
    div x3, other arithmetic, relax(): return (right_hand + inflow) / diagonal  9.84 us
    ppermute x4, starting transfers between devices, padded_2(): lax.ppermute(lax.slice_in_dim(block, block.shape[dim] - width, None, axis...  8.46 us
    reduce_sum x1, other arithmetic, local(): jnp.sum(conduct, axis=0)  7.77 us
    add x2, other arithmetic, local(): summed + lax.ppermute(summed, 'layer', [(dev, dev ^ hop) for dev in range...  7.52 us
    mul x1, other arithmetic, local(): harmonic(conduct, side_conduct) * (cell_pressure - side_pressure)  7.44 us
  transfers between devices with their start and end apart: 11, of which 4 were waited for; matrix products, arithmetic and copies ran while one was open for 12% of the time, Pallas kernels for 0%

profile of v1, /device:TPU:4, one launch (start us, length us, event | category | flops | bytes accessed | tf_op | source)
XLA Modules:
  0.0 220.7 jit_solution(15150886650092543474)
XLA Ops:
  0.6 7.8 %fusion.60 = (f32[512,512]{1,0:T(8,128)S(1)}, f32[512,512]{1,0:T(8,128)S(1)}, f32[4,512,512]{2,1,0:T(8,128)}) fusion(s32[512,512]{1,0:T(8,128)} %param.14, s32[512,512]{1,0:T(8,128)} %param.13, s32[4]{0:T(128)S(1)} %iota_add_fusion.1, f32[4]{0:T(128)} %param.12, f32[4,512,512]{2,1,0:T(8,128)} %param.10, f32[4,512,512]{2,1,0:T(8,128)} %param.11), kind=kLoop, calls=%fused_computation.139 | loop fusion | flops 8912896 | bytes 16777248 | tf_op jit(solution)/shard_map/reduce_sum | solution.py:113
  9.4 1.5 pad_maximum_fusion.2
  10.9 1.6 collective-permute-start
  13.2 1.9 collective-permute-start.4
  15.2 4.5 %collective-permute-start.5 = (f32[1,512]{1,0:T(1,128)S(1)}, f32[1,512]{1,0:T(1,128)S(1)}, u32[]{:S(2)}, u32[]{:S(2)}) collective-permute-start(f32[1,512]{1,0:T(1,128)S(1)} %get-tuple-element.192), channel_id=1, source_target_pairs={{4,0},{8,4},{12,8},{16,12},{20,16},{24,20},{28,24},{5,1},{9,5},{13... | collective-permute-start | bytes 6152 | tf_op jit(solution)/shard_map/ppermute | solution.py:21
  21.2 42.7 %all-reduce.8 = f32[16]{0:T(128)S(1)} all-reduce(f32[16]{0:T(128)S(1)} %dynamic-update-slice), channel_id=1, replica_groups=mesh['area'=8,'layer'=4] {'layer'}, use_global_device_ids=true, to_apply=%add.8 | all-reduce | flops 16 | bytes 128
  63.9 4.0 %fusion.59 = f32[2,512,512]{2,1,0:T(8,128)} fusion(f32[2,512,512]{2,1,0:T(8,128)} %collective-permute-done, f32[1,512,512]{2,1,0:T(8,128)} %bitcast.93, f32[1,512,512]{2,1,0:T(8,128)} %bitcast.90), kind=kLoop, calls=%fused_computation.138 | loop fusion | flops 1048576 | bytes 6291456 | tf_op jit(solution)/shard_map/add | solution.py:117
  67.9 12.6 %while.16 = (s32[]{:T(128)}, f32[512,512]{1,0:T(8,128)S(1)}, f32[512,512]{1,0:T(8,128)}, s32[512,512]{1,0:T(8,128)S(1)}, s32[512,512]{1,0:T(8,128)S(1)}, /*index...) while((s32[]{:T(128)}, f32[512,512]{1,0:T(8,128)S(1)}, ...), condition=%wide.region_5.6_spmd.clone, body=%wide.region_2.5_spmd.clone.sunk | while | flops 8912915 | bytes 18874700 | solution.py:98
  81.2 78.0 %collective-permute-done.1 = f32[2,512,512]{2,1,0:T(8,128)} collective-permute-done((f32[2,512,512]{2,1,0:T(8,128)}, f32[2,512,512]{2,1,0:T(8,128)}, u32[]{:S(2)}, u32[]{:S(2)}) %collective-permute-start.1) | collective-permute-done | bytes 2097184 | tf_op jit(solution)/shard_map/ppermute | solution.py:117
  159.2 3.6 %fusion.67 = f32[2,512,512]{2,1,0:T(8,128)S(1)} fusion(f32[2,512,512]{2,1,0:T(8,128)} %collective-permute-done.1, f32[2,512,512]{2,1,0:T(8,128)} %collective-permute-done, f32[1,512,512]{2,1,0:T(8,128)} %bitcast.94, f32[1,512,512]{2,1,0:T(8,128)} %bitcast.91), kind=kLoop, calls=%fused_computation.143 | loop fusion | flops 1572864 | bytes 8388608 | tf_op jit(solution)/shard_map/add | solution.py:117
  162.7 2.1 collective-permute-start.2
  164.8 4.5 %collective-permute-start.3 = (f32[3,1,512]{2,1,0:T(1,128)S(1)}, f32[3,1,512]{2,1,0:T(1,128)S(1)}, u32[]{:S(2)}, u32[]{:S(2)}) collective-permute-start(f32[3,1,512]{2,1,0:T(1,128)S(1)} %get-tuple-element.186), channel_id=1, source_target_pairs={{4,0},{8,4},{12,8},{16,12},{20,16},{24,20},{28,24},{5,1},{9,5},{13... | collective-permute-start | bytes 18440 | tf_op jit(solution)/shard_map/ppermute | solution.py:21
  172.6 6.4 %fusion.46 = (f32[512,512]{1,0:T(8,128)S(1)}, f32[512,512]{1,0:T(8,128)S(1)}, f32[512,512]{1,0:T(8,128)S(1)}, f32[512,512]{1,0:T(8,128)S(1)}) fusion(f32[514,514]{1,0:T(8,128)S(1)} %select_maximum_fusion.4, f32[1,512]{1,0:T(1,128)S(1)} %collective-permute-done.5, f32[512,512]{1,0:T(8,128)S(1)} %copy-done.10, f32[1,512]{1,0:T(1,128)S(1)} %collective-permute-done.4, ...), kind=kLoop, calls=%fused_computation.98 | loop fusion | flops 20709376 | bytes 21037056 | tf_op jit(solution)/shard_map/div | solution.py:81
  179.1 2.6 %collective-permute-start.6 = (f32[1,512]{1,0:T(1,128)S(1)}, f32[1,512]{1,0:T(1,128)S(1)}, u32[]{:S(2)}, u32[]{:S(2)}) collective-permute-start(f32[1,512]{1,0:T(1,128)S(1)} %get-tuple-element.189), channel_id=1, source_target_pairs={{0,4},{4,8},{8,12},{12,16},{16,20},{20,24},{24,28},{1,5},{5,9},{9,... | collective-permute-start | bytes 6152 | tf_op jit(solution)/shard_map/ppermute | solution.py:18
  181.7 3.9 %collective-permute-start.7 = (f32[1,512]{1,0:T(1,128)S(1)}, f32[1,512]{1,0:T(1,128)S(1)}, u32[]{:S(2)}, u32[]{:S(2)}) collective-permute-start(f32[1,512]{1,0:T(1,128)S(1)} %get-tuple-element.190), channel_id=1, source_target_pairs={{4,0},{8,4},{12,8},{16,12},{20,16},{24,20},{28,24},{5,1},{9,5},{13... | collective-permute-start | bytes 6152 | tf_op jit(solution)/shard_map/ppermute | solution.py:21
  187.3 1.7 fusion.39
  189.0 1.9 collective-permute-start.8
  191.0 4.7 %collective-permute-start.9 = (f32[1,512]{1,0:T(1,128)S(1)}, f32[1,512]{1,0:T(1,128)S(1)}, u32[]{:S(2)}, u32[]{:S(2)}) collective-permute-start(f32[1,512]{1,0:T(1,128)S(1)} %get-tuple-element.188), channel_id=1, source_target_pairs={{4,0},{8,4},{12,8},{16,12},{20,16},{24,20},{28,24},{5,1},{9,5},{13... | collective-permute-start | bytes 6152 | tf_op jit(solution)/shard_map/ppermute | solution.py:21
  197.3 1.7 fusion.32
  199.0 2.2 multiply_add_fusion
  201.2 4.5 %collective-permute-start.10 = (f32[2,4,512]{2,0,1:T(2,128)S(1)}, f32[2,4,512]{2,0,1:T(2,128)S(1)}, u32[]{:S(2)}, u32[]{:S(2)}) collective-permute-start(f32[2,4,512]{2,0,1:T(2,128)S(1)} %pad_maximum_fusion.13), channel_id=1, source_target_pairs={{4,0},{8,4},{12,8},{16,12},{20,16},{24,20},{28,24},{5,1},{9,5},{13... | collective-permute-start | bytes 49160 | tf_op jit(solution)/shard_map/ppermute | solution.py:29
  207.5 3.1 %slice.283 = f32[4,512,511]{2,1,0:T(8,128)} slice(f32[4,512,512]{2,1,0:T(8,128)S(1)} %multiply_add_fusion), slice={[0:4], [0:512], [1:512]} | slice | bytes 8372224 | tf_op jit(solution)/shard_map/slice | solution.py:137
  210.7 2.5 %slice.280 = f32[4,511,512]{2,1,0:T(8,128)} slice(f32[4,512,512]{2,1,0:T(8,128)S(1)} %multiply_add_fusion), slice={[0:4], [1:512], [0:512]} | slice | bytes 8372224 | tf_op jit(solution)/shard_map/slice | solution.py:134
  213.2 7.4 %fusion.3 = (f32[4,512,512]{2,1,0:T(8,128)}, f32[4,512,512]{2,1,0:T(8,128)}) fusion(f32[4,512,512]{2,1,0:T(8,128)S(1)} %multiply_add_fusion, f32[4,512,511]{2,1,0:T(8,128)} %slice.283, f32[4,512,512]{2,1,0:T(8,128)S(1)} %copy-done.1, f32[4,512,511]{2,1,0:T(8,128)S(1)} %slice.282, f32[4,1,512]{2,1,0:T(1,128)S(1)} %get-tuple-element.194, ...), kind=kLoop, calls=%fused_computation.14 | loop fusion | flops 17825792 | bytes 33538048 | tf_op jit(solution)/shard_map/mul | solution.py:138
  (94 shorter events, 24.0 us)
Async XLA Ops:
  8.4 2.5 %copy-start.8 = (f32[512,512]{1,0:T(8,128)}, f32[512,512]{1,0:T(8,128)S(1)}, u32[]{:S(2)}) copy-start(f32[512,512]{1,0:T(8,128)S(1)} %get-tuple-element.157) | copy-start | bytes 3145732
  8.4 11.3 %copy-start.13 = (u32[32]{0:T(128)S(1)}, u32[32]{0:T(128)}, u32[]{:S(2)}) copy-start(u32[32]{0:T(128)} %constant.82) | copy-start | bytes 388
  8.4 12.6 %copy-start.12 = (f32[4]{0:T(128)S(1)}, f32[4]{0:T(128)}, u32[]{:S(2)}) copy-start(f32[4]{0:T(128)} %param.12) | copy-start | bytes 52
  10.9 57.0 %copy-start.2 = (s32[512,512]{1,0:T(8,128)S(1)}, s32[512,512]{1,0:T(8,128)}, u32[]{:S(2)}) copy-start(s32[512,512]{1,0:T(8,128)} %param.13) | copy-start | bytes 3145732
  10.9 57.0 %copy-start.3 = (s32[512,512]{1,0:T(8,128)S(1)}, s32[512,512]{1,0:T(8,128)}, u32[]{:S(2)}) copy-start(s32[512,512]{1,0:T(8,128)} %param.14) | copy-start | bytes 3145732
  10.9 53.0 %collective-permute-start = (f32[2,512,512]{2,1,0:T(8,128)}, f32[2,512,512]{2,1,0:T(8,128)}, u32[]{:S(2)}, u32[]{:S(2)}) collective-permute-start(f32[2,512,512]{2,1,0:T(8,128)} %pad_maximum_fusion.2), channel_id=1, source_target_pairs={{0,1},{1,0},{2,3},{3,2},{4,5},{5,4},{6,7},{7,6},{8,9},{9,8},{10,11... | collective-permute-start | bytes 6291464 | tf_op jit(solution)/shard_map/ppermute | solution.py:117
  13.2 156.1 %collective-permute-start.4 = (f32[1,512]{1,0:T(1,128)S(1)}, f32[1,512]{1,0:T(1,128)S(1)}, u32[]{:S(2)}, u32[]{:S(2)}) collective-permute-start(f32[1,512]{1,0:T(1,128)S(1)} %get-tuple-element.191), channel_id=1, source_target_pairs={{0,4},{4,8},{8,12},{12,16},{16,20},{20,24},{24,28},{1,5},{5,9},{9,... | collective-permute-start | bytes 6152 | tf_op jit(solution)/shard_map/ppermute | solution.py:18
  15.2 154.2 %collective-permute-start.5 = (f32[1,512]{1,0:T(1,128)S(1)}, f32[1,512]{1,0:T(1,128)S(1)}, u32[]{:S(2)}, u32[]{:S(2)}) collective-permute-start(f32[1,512]{1,0:T(1,128)S(1)} %get-tuple-element.192), channel_id=1, source_target_pairs={{4,0},{8,4},{12,8},{16,12},{20,16},{24,20},{28,24},{5,1},{9,5},{13... | collective-permute-start | bytes 6152 | tf_op jit(solution)/shard_map/ppermute | solution.py:21
  67.9 91.2 %collective-permute-start.1 = (f32[2,512,512]{2,1,0:T(8,128)}, f32[2,512,512]{2,1,0:T(8,128)}, u32[]{:S(2)}, u32[]{:S(2)}) collective-permute-start(f32[2,512,512]{2,1,0:T(8,128)} %fusion.59), channel_id=1, source_target_pairs={{0,2},{1,3},{2,0},{3,1},{4,6},{5,7},{6,4},{7,5},{8,10},{9,11},{10,... | collective-permute-start | bytes 6291464 | tf_op jit(solution)/shard_map/ppermute | solution.py:117
  67.9 1.4 copy-start.4
  71.1 1.4 copy-start.4
  74.3 1.4 copy-start.4
  162.7 6.7 %copy-start.10 = (f32[512,512]{1,0:T(8,128)S(1)}, f32[512,512]{1,0:T(8,128)}, u32[]{:S(2)}) copy-start(f32[512,512]{1,0:T(8,128)} %param.17) | copy-start | bytes 3145732
  162.7 7.1 %collective-permute-start.2 = (f32[3,1,512]{2,1,0:T(1,128)S(1)}, f32[3,1,512]{2,1,0:T(1,128)S(1)}, u32[]{:S(2)}, u32[]{:S(2)}) collective-permute-start(f32[3,1,512]{2,1,0:T(1,128)S(1)} %get-tuple-element.185), channel_id=1, source_target_pairs={{0,4},{4,8},{8,12},{12,16},{16,20},{20,24},{24,28},{1,5},{5,9},{9,... | collective-permute-start | bytes 18440 | tf_op jit(solution)/shard_map/ppermute | solution.py:18
  164.8 5.9 %collective-permute-start.3 = (f32[3,1,512]{2,1,0:T(1,128)S(1)}, f32[3,1,512]{2,1,0:T(1,128)S(1)}, u32[]{:S(2)}, u32[]{:S(2)}) collective-permute-start(f32[3,1,512]{2,1,0:T(1,128)S(1)} %get-tuple-element.186), channel_id=1, source_target_pairs={{4,0},{8,4},{12,8},{16,12},{20,16},{24,20},{28,24},{5,1},{9,5},{13... | collective-permute-start | bytes 18440 | tf_op jit(solution)/shard_map/ppermute | solution.py:21
  171.1 1.5 copy-start.11
  172.6 12.9 %copy-start.6 = (f32[512,512]{1,0:T(8,128)S(1)}, f32[512,512]{1,0:T(8,128)}, u32[]{:S(2)}) copy-start(f32[512,512]{1,0:T(8,128)} %get-tuple-element.129) | copy-start | bytes 3145732
  179.1 7.2 %collective-permute-start.6 = (f32[1,512]{1,0:T(1,128)S(1)}, f32[1,512]{1,0:T(1,128)S(1)}, u32[]{:S(2)}, u32[]{:S(2)}) collective-permute-start(f32[1,512]{1,0:T(1,128)S(1)} %get-tuple-element.189), channel_id=1, source_target_pairs={{0,4},{4,8},{8,12},{12,16},{16,20},{20,24},{24,28},{1,5},{5,9},{9,... | collective-permute-start | bytes 6152 | tf_op jit(solution)/shard_map/ppermute | solution.py:18
  181.7 5.2 %collective-permute-start.7 = (f32[1,512]{1,0:T(1,128)S(1)}, f32[1,512]{1,0:T(1,128)S(1)}, u32[]{:S(2)}, u32[]{:S(2)}) collective-permute-start(f32[1,512]{1,0:T(1,128)S(1)} %get-tuple-element.190), channel_id=1, source_target_pairs={{4,0},{8,4},{12,8},{16,12},{20,16},{24,20},{28,24},{5,1},{9,5},{13... | collective-permute-start | bytes 6152 | tf_op jit(solution)/shard_map/ppermute | solution.py:21
  187.3 8.4 %copy-start.1 = (f32[4,512,512]{2,1,0:T(8,128)S(1)}, f32[4,512,512]{2,1,0:T(8,128)}, u32[]{:S(2)}) copy-start(f32[4,512,512]{2,1,0:T(8,128)} %get-tuple-element.176) | copy-start | bytes 12582916
  189.0 6.7 %collective-permute-start.8 = (f32[1,512]{1,0:T(1,128)S(1)}, f32[1,512]{1,0:T(1,128)S(1)}, u32[]{:S(2)}, u32[]{:S(2)}) collective-permute-start(f32[1,512]{1,0:T(1,128)S(1)} %get-tuple-element.187), channel_id=1, source_target_pairs={{0,4},{4,8},{8,12},{12,16},{16,20},{20,24},{24,28},{1,5},{5,9},{9,... | collective-permute-start | bytes 6152 | tf_op jit(solution)/shard_map/ppermute | solution.py:18
  191.0 5.8 %collective-permute-start.9 = (f32[1,512]{1,0:T(1,128)S(1)}, f32[1,512]{1,0:T(1,128)S(1)}, u32[]{:S(2)}, u32[]{:S(2)}) collective-permute-start(f32[1,512]{1,0:T(1,128)S(1)} %get-tuple-element.188), channel_id=1, source_target_pairs={{4,0},{8,4},{12,8},{16,12},{20,16},{24,20},{28,24},{5,1},{9,5},{13... | collective-permute-start | bytes 6152 | tf_op jit(solution)/shard_map/ppermute | solution.py:21
  201.2 12.0 %copy-start = (f32[4,512,512]{2,1,0:T(8,128)}, f32[4,512,512]{2,1,0:T(8,128)S(1)}, u32[]{:S(2)}) copy-start(f32[4,512,512]{2,1,0:T(8,128)S(1)} %multiply_add_fusion) | copy-start | bytes 12582916
  201.2 12.0 %collective-permute-start.10 = (f32[2,4,512]{2,0,1:T(2,128)S(1)}, f32[2,4,512]{2,0,1:T(2,128)S(1)}, u32[]{:S(2)}, u32[]{:S(2)}) collective-permute-start(f32[2,4,512]{2,0,1:T(2,128)S(1)} %pad_maximum_fusion.13), channel_id=1, source_target_pairs={{4,0},{8,4},{12,8},{16,12},{20,16},{24,20},{28,24},{5,1},{9,5},{13... | collective-permute-start | bytes 49160 | tf_op jit(solution)/shard_map/ppermute | solution.py:29
  (7 other events, 7.6 us)
